TPU v7x, 32 devices: a whole 2x2x4 slice. The times are simulated.
32 devices in a mesh: blocks: 2 (over y), rows: 4 (over z), cols: 4 (over x, core).
Axes of the slice: x: 2, y: 2, z: 4, core: 2. Of those that a mesh axis runs over, the one named last changes fastest.
Arguments:
- sens_tiles: bfloat16 [128, 1024, 256], P(('blocks', 'rows'), 'cols'), parts along dimension 0, may hold values from -10.606602 to 10.606602, as said below
- tile_coords: int32 [128, 8], P(('blocks', 'rows'), 'cols'), parts along dimension 0, may hold values from 0 to 7, as said below
- tile_counts: int32 [8, 4], P(('blocks', 'rows'), 'cols'), parts along dimension 0, may hold values from 3 to 16, as said below
- data_vec: float32 [192, 4096], P('blocks', 'rows'), parts along dimension 0, may hold values from -6 to 6
- cell_vec: float32 [192, 8192], P('blocks', 'cols'), parts along dimension 0, may hold values from -6 to 6
- alpha_now: float32 [192], P('blocks'), parts along dimension 0, may hold values from 0.5 to 2
Outputs:
- data_next: float32 [192, 4096], P('blocks', 'rows'), parts along dimension 0
- cell_next: float32 [192, 8192], P('blocks', 'cols'), parts along dimension 0
- beta_next: float32 [192], P('blocks'), parts along dimension 0
- alpha_next: float32 [192], P('blocks'), parts along dimension 0
There are 2 independent parts, one for each index of `blocks`. A program takes and returns all parts, laid end to end along the dimension named above; each array names one. Nothing has to cross between parts.
Inputs may be any that keep to these rules, and one draw needn't show every extreme that they name: `sens_tiles`: entries of the tiles; slots at or beyond a device's count hold values that belong to no tile. `tile_coords`: within one device all 16 slots name distinct (row tile, column tile) pairs; the first entry of a pair is below 4, the second below 8. `tile_counts`: every data-row band has one device whose count is 16.
All inputs are finite; a program needn't handle non-finite values.
Results may differ from a plain program's by a relative error of at most 0.0043.
Values sent between devices are 32-bit elements; how exact they have to be, the bound alone decides.
No kernel may reach another device: no remote copies, remote signals or barrier semaphores. Data moves between devices by JAX's collectives and lax.ppermute only.
A program may use at most 64 MiB of HBM per device.

v0:
```python
import jax
import jax.numpy as jnp
from jax import lax
from jax.sharding import PartitionSpec as P

EPSILON = 1e-06


def listed_mask(sens_tiles, listed_count):
    return (jnp.arange(sens_tiles.shape[0], dtype=jnp.int32) < listed_count).astype(jnp.float32)


def forward_sweep(sens_tiles, tile_coords, listed_count, cell_low, row_tiles):
    samples = cell_low.shape[0]
    tile_size = sens_tiles.shape[1]
    listed = listed_mask(sens_tiles, listed_count)
    blocks = cell_low.reshape(samples, cell_low.shape[1] // tile_size, tile_size)
    picked = jnp.take(blocks, tile_coords[:, 1], axis=1)
    contrib = jnp.einsum("ktj,tij->kti", picked, sens_tiles, preferred_element_type=jnp.float32)
    spread = jax.nn.one_hot(tile_coords[:, 0], row_tiles, dtype=jnp.float32) * listed[:, None]
    placed = jnp.einsum("kti,tr->kri", contrib, spread, precision=lax.Precision.HIGHEST)
    return placed.reshape(samples, row_tiles * tile_size)


def adjoint_sweep(sens_tiles, tile_coords, listed_count, data_low, col_tiles):
    samples = data_low.shape[0]
    tile_size = sens_tiles.shape[1]
    listed = listed_mask(sens_tiles, listed_count)
    blocks = data_low.reshape(samples, data_low.shape[1] // tile_size, tile_size)
    picked = jnp.take(blocks, tile_coords[:, 0], axis=1)
    contrib = jnp.einsum("kti,tij->ktj", picked, sens_tiles, preferred_element_type=jnp.float32)
    spread = jax.nn.one_hot(tile_coords[:, 1], col_tiles, dtype=jnp.float32) * listed[:, None]
    placed = jnp.einsum("ktj,ts->ksj", contrib, spread, precision=lax.Precision.HIGHEST)
    return placed.reshape(samples, col_tiles * tile_size)


def per_device(sens_tiles, tile_coords, tile_counts, data_vec, cell_vec, alpha_now):
    tile_size = sens_tiles.shape[1]
    row_tiles = data_vec.shape[1] // tile_size
    col_tiles = cell_vec.shape[1] // tile_size
    listed_count = tile_counts[0, 0]
    data_total = data_vec.shape[1] * lax.axis_size("rows")
    cell_total = cell_vec.shape[1] * lax.axis_size("cols")
    cell_low = cell_vec.astype(jnp.bfloat16)
    partial_rows = forward_sweep(sens_tiles, tile_coords, listed_count, cell_low, row_tiles)
    row_full = lax.psum(partial_rows, "cols")
    residual = row_full - alpha_now[:, None] * data_vec
    squares = lax.psum(jnp.sum(residual * residual, axis=1), "rows")
    beta_next = jnp.sqrt(squares / data_total + EPSILON)
    data_next = residual / beta_next[:, None]
    data_low = data_next.astype(jnp.bfloat16)
    partial_cells = adjoint_sweep(sens_tiles, tile_coords, listed_count, data_low, col_tiles)
    cell_full = lax.psum(partial_cells, "rows")
    fresh = cell_full - beta_next[:, None] * cell_vec
    sumsq = lax.psum(jnp.sum(fresh * fresh, axis=1), "cols")
    alpha_next = jnp.sqrt(sumsq / cell_total + EPSILON)
    cell_next = fresh / alpha_next[:, None]
    return (data_next, cell_next, beta_next, alpha_next)


def solution(mesh):
    placed = (
        P(("blocks", "rows"), "cols", None),
        P(("blocks", "rows"), "cols"),
        P(("blocks", "rows"), "cols"),
        P("blocks", "rows"),
        P("blocks", "cols"),
        P("blocks"),
    )
    return jax.shard_map(
        per_device,
        mesh=mesh,
        in_specs=placed,
        out_specs=(P("blocks", "rows"), P("blocks", "cols"), P("blocks"), P("blocks")),
        check_vma=False,
    )
```

profile of v0, /device:TPU:0, one launch (start us, length us, event | category | flops | bytes accessed | tf_op | source)
XLA Modules:
  0.0 127.0 jit_solution(8777433551403314318)
XLA Ops:
  7.2 0.0 copy-start
  7.2 0.0 all-reduce.3.cloned.1.call-start
  7.2 0.8 and_bitcast_fusion
  8.1 0.8 slice_bitcast_fusion
  9.5 1.2 convert_element_type.19
  10.7 0.6 gather_fusion
  11.3 0.0 copy-done
  11.3 0.8 convolution_bitcast_fusion.1
  12.1 0.0 copy-start.2
  12.1 0.0 copy-start.4
  12.1 1.7 %fusion.2 = f32[4,96,256]{2,0,1:T(4,128)S(1)} fusion(f32[96,16,256]{2,0,1:T(8,128)S(1)} %convolution_bitcast_fusion.1, f32[16]{0:T(128)S(1)} %compare_convert_fusion, s32[16]{0:T(128)S(1)} %get-tuple-element.9), kind=kOutput, calls=%fused_computation.4 | convolution fusion | flops 18874496 | bytes 1966208 | tf_op jit(solution)/shard_map/kti,tr->kri/dot_general | solution.py:21
  13.9 0.8 copy.16
  14.7 0.0 all-reduce.3.cloned.1.call-update
  14.7 0.0 all-reduce.5.cloned.1.call-start
  14.8 35.6 %all-reduce.3.cloned.1.call-done = f32[96,1024]{1,0:T(8,128)} async-done(((f32[96,1024]{1,0:T(8,128)}), f32[96,1024]{1,0:T(8,128)}) %all-reduce.3.cloned.1.call-update) | async-done | bytes 393232 | tf_op jit(solution)/shard_map/psum | solution.py:46
  50.4 0.0 copy-done.2
  50.4 0.0 copy-done.4
  50.4 1.2 multiply_reduce_fusion.1
  51.6 11.7 %psum.29 = f32[96]{0:T(128)S(1)} all-reduce(f32[96]{0:T(128)S(1)} %multiply_reduce_fusion.1), channel_id=1, replica_groups=mesh['blocks'=2,'rows'=4,'cols'=4] {'rows'}, use_global_device_ids=true, to_apply=%region_2.3 | all-reduce | flops 96 | bytes 768 | tf_op jit(solution)/shard_map/psum | solution.py:48
  63.3 0.0 copy-start.3
  63.3 1.9 %fusion.28 = (bf16[96,1024]{1,0:T(8,128)(2,1)S(1)}, f32[96,1024]{1,0:T(8,128)}) fusion(f32[96]{0:T(128)S(1)} %add_sqrt_fusion.1, f32[96,1024]{1,0:T(8,128)} %all-reduce.3.cloned.1.call-done, f32[96,1024]{1,0:T(8,128)S(1)} %copy-done.2, f32[96]{0:T(128)S(1)} %copy-done.4), kind=kLoop, calls=%fused_computation.53 | loop fusion | flops 393216 | bytes 1377024 | tf_op jit(solution)/shard_map/convert_element_type | solution.py:51
  65.2 0.6 gather_fusion.1
  65.8 0.5 convolution_bitcast_fusion
  66.3 1.7 %fusion = f32[8,96,256]{2,0,1:T(8,128)S(1)} fusion(f32[96,16,256]{2,0,1:T(8,128)S(1)} %convolution_bitcast_fusion, f32[16]{0:T(128)S(1)} %compare_convert_fusion, s32[16]{0:T(128)S(1)} %get-tuple-element.6), kind=kOutput, calls=%fused_computation.2 | convolution fusion | flops 37748992 | bytes 2359424 | tf_op jit(solution)/shard_map/ktj,ts->ksj/dot_general | solution.py:33
  68.1 0.0 copy-start.1
  68.1 1.1 copy.17
  69.2 0.0 all-reduce.5.cloned.1.call-update
  69.2 41.3 %all-reduce.5.cloned.1.call-done = f32[96,2048]{1,0:T(8,128)} async-done(((f32[96,2048]{1,0:T(8,128)}), f32[96,2048]{1,0:T(8,128)}) %all-reduce.5.cloned.1.call-update) | async-done | bytes 786448 | tf_op jit(solution)/shard_map/psum | solution.py:53
  110.5 0.0 copy-done.1
  110.5 1.4 %multiply_reduce_fusion = f32[96]{0:T(128)S(1)} fusion(f32[96,2048]{1,0:T(8,128)} %all-reduce.5.cloned.1.call-done, f32[96,2048]{1,0:T(8,128)S(1)} %copy-done.1, f32[96]{0:T(128)S(1)} %add_sqrt_fusion.1), kind=kLoop, calls=%fused_computation.12 | loop fusion | flops 786336 | bytes 1573632 | tf_op jit(solution)/shard_map/reduce_sum | solution.py:55
  111.9 6.0 %psum.31 = f32[96]{0:T(128)S(1)} all-reduce(f32[96]{0:T(128)S(1)} %multiply_reduce_fusion), channel_id=1, replica_groups=mesh['blocks'=2,'rows'=4,'cols'=4] {'cols'}, use_global_device_ids=true, to_apply=%region_5.6 | all-reduce | flops 96 | bytes 768 | tf_op jit(solution)/shard_map/psum | solution.py:55
  118.0 0.0 copy-done.3
  118.0 0.0 copy-start.5
  118.0 2.2 %broadcast_divide_fusion = f32[96,2048]{1,0:T(8,128)} fusion(f32[96]{0:T(128)S(1)} %add_sqrt_fusion, f32[96,2048]{1,0:T(8,128)} %all-reduce.5.cloned.1.call-done, f32[96,2048]{1,0:T(8,128)S(1)} %copy-done.1, f32[96]{0:T(128)S(1)} %add_sqrt_fusion.1), kind=kLoop, calls=%fused_computation.19 | loop fusion | flops 589824 | bytes 2360064 | tf_op jit(solution)/shard_map/div | solution.py:57
  120.2 0.0 copy-done.5
  (6 shorter events, 0.1 us)
Async XLA Ops:
  7.2 4.2 %copy-start = (bf16[16,256,256]{2,1,0:T(8,128)(2,1)S(1)}, bf16[16,256,256]{2,1,0:T(8,128)(2,1)}, u32[]{:S(2)}) copy-start(bf16[16,256,256]{2,1,0:T(8,128)(2,1)} %param.6) | copy-start | bytes 6291460
  7.2 43.2 %all-reduce.3.cloned.1.call-start = ((), (), s32[]{:S(2)}) async-start(), calls=%async_computation | async-start | bytes 786432 | tf_op jit(solution)/shard_map/psum | solution.py:46
  12.1 38.3 %copy-start.2 = (f32[96,1024]{1,0:T(8,128)S(1)}, f32[96,1024]{1,0:T(8,128)}, u32[]{:S(2)}) copy-start(f32[96,1024]{1,0:T(8,128)} %param.9) | copy-start | bytes 1179652
  12.1 38.3 %copy-start.4 = (f32[96]{0:T(128)S(1)}, f32[96]{0:T(128)}, u32[]{:S(2)}) copy-start(f32[96]{0:T(128)} %param.11) | copy-start | bytes 1156
  14.7 95.8 %all-reduce.5.cloned.1.call-start = ((), (), s32[]{:S(2)}) async-start(), calls=%async_computation.1 | async-start | bytes 1572864 | tf_op jit(solution)/shard_map/psum | solution.py:53
  63.3 54.7 %copy-start.3 = (f32[96]{0:T(128)}, f32[96]{0:T(128)S(1)}, u32[]{:S(2)}) copy-start(f32[96]{0:T(128)S(1)} %add_sqrt_fusion.1) | copy-start | bytes 1156
  68.1 42.5 %copy-start.1 = (f32[96,2048]{1,0:T(8,128)S(1)}, f32[96,2048]{1,0:T(8,128)}, u32[]{:S(2)}) copy-start(f32[96,2048]{1,0:T(8,128)} %param.10) | copy-start | bytes 2359300
  118.0 2.2 %copy-start.5 = (f32[96]{0:T(128)}, f32[96]{0:T(128)S(1)}, u32[]{:S(2)}) copy-start(f32[96]{0:T(128)S(1)} %add_sqrt_fusion) | copy-start | bytes 1156
Sparse Core Ops, SparseCore 0:
  14.8 35.5 all-reduce.2
  69.3 41.1 all-reduce.4
where the time goes:
time: 127 us
  waiting for transfers between devices  77 us (61%)
  blocking collectives  17.7 us (14%)
  between operations  14.8 us (12%)
  other arithmetic  9.5 us (7%)
  matrix products  4.7 us (4%)
  local copies, waits for them, and re-layouts  3.22 us (3%)
    psum x1, waiting for transfers between devices, per_device(): cell_full = lax.psum(partial_cells, 'rows')  41.3 us
    psum x1, waiting for transfers between devices, per_device(): row_full = lax.psum(partial_rows, 'cols')  35.6 us
    psum x1, blocking collectives, per_device(): squares = lax.psum(jnp.sum(residual * residual, axis=1), 'rows')  11.7 us
    psum x1, blocking collectives, per_device(): sumsq = lax.psum(jnp.sum(fresh * fresh, axis=1), 'cols')  6.04 us
  transfers between devices with their start and end apart: 2, of which 2 were waited for; matrix products, arithmetic and copies ran while one was open for 0% of the time, Pallas kernels for 0%

commit v1 on v0

--- a/solution.py
+++ b/solution.py
@@ -50,7 +50,7 @@
     data_next = residual / beta_next[:, None]
     data_low = data_next.astype(jnp.bfloat16)
     partial_cells = adjoint_sweep(sens_tiles, tile_coords, listed_count, data_low, col_tiles)
-    cell_full = lax.psum(partial_cells, "rows")
+    cell_full = jnp.sum(lax.all_gather(partial_cells, "rows"), axis=0)
     fresh = cell_full - beta_next[:, None] * cell_vec
     sumsq = lax.psum(jnp.sum(fresh * fresh, axis=1), "cols")
     alpha_next = jnp.sqrt(sumsq / cell_total + EPSILON)

time: 127 us -> 150 us (1.18)
  waiting for transfers between devices: 77 us -> 96.5 us
  other arithmetic: 9.5 us -> 12.6 us
    all_gather x0 -> x1, waiting for transfers between devices: none -> 60.8 us  [per_device(): cell_full = jnp.sum(lax.all_gather(partial_cells, 'rows'), axis=0)]
    psum x1 -> x0, waiting for transfers between devices: 41.3 us -> none  [per_device(): cell_full = lax.psum(partial_cells, 'rows')]
    reduce_sum x0 -> x1, other arithmetic: none -> 3.05 us  [per_device(): cell_full = jnp.sum(lax.all_gather(partial_cells, 'rows'), axis=0)]
where the time goes in v1:
time: 150 us
  waiting for transfers between devices  96.5 us (64%)
  blocking collectives  18.1 us (12%)
  between operations  14.8 us (10%)
  other arithmetic  12.6 us (8%)
  matrix products  4.7 us (3%)
  local copies, waits for them, and re-layouts  3.09 us (2%)
    all_gather x1, waiting for transfers between devices, per_device(): cell_full = jnp.sum(lax.all_gather(partial_cells, 'rows'), axis=0)  60.8 us
    psum x1, waiting for transfers between devices, per_device(): row_full = lax.psum(partial_rows, 'cols')  35.6 us
    psum x1, blocking collectives, per_device(): squares = lax.psum(jnp.sum(residual * residual, axis=1), 'rows')  11.7 us
    psum x1, blocking collectives, per_device(): sumsq = lax.psum(jnp.sum(fresh * fresh, axis=1), 'cols')  6.4 us
    reduce_sum x1, other arithmetic, per_device(): cell_full = jnp.sum(lax.all_gather(partial_cells, 'rows'), axis=0)  3.05 us
  transfers between devices with their start and end apart: 2, of which 2 were waited for; matrix products, arithmetic and copies ran while one was open for 0% of the time, Pallas kernels for 0%

profile of v1, /device:TPU:0, one launch (start us, length us, event | category | flops | bytes accessed | tf_op | source)
XLA Modules:
  0.0 149.8 jit_solution(15041443913796763184)
XLA Ops:
  7.2 0.0 copy-start
  7.2 0.0 all-reduce.2.cloned.1.call-start
  7.2 0.8 and_bitcast_fusion
  8.1 0.8 slice_bitcast_fusion
  9.5 1.2 convert_element_type.19
  10.7 0.6 gather_fusion
  11.3 0.0 copy-done
  11.3 0.8 convolution_bitcast_fusion.1
  12.1 0.0 copy-start.2
  12.1 0.0 copy-start.4
  12.1 1.7 %fusion.2 = f32[4,96,256]{2,0,1:T(4,128)S(1)} fusion(f32[96,16,256]{2,0,1:T(8,128)S(1)} %convolution_bitcast_fusion.1, f32[16]{0:T(128)S(1)} %compare_convert_fusion, s32[16]{0:T(128)S(1)} %get-tuple-element.9), kind=kOutput, calls=%fused_computation.4 | convolution fusion | flops 18874496 | bytes 1966208 | tf_op jit(solution)/shard_map/kti,tr->kri/dot_general | solution.py:21
  13.9 0.8 copy.20
  14.7 0.0 all-reduce.2.cloned.1.call-update
  14.7 0.0 all-gather.2.cloned.1.call-start
  14.8 35.6 %all-reduce.2.cloned.1.call-done = f32[96,1024]{1,0:T(8,128)} async-done(((f32[96,1024]{1,0:T(8,128)}), f32[96,1024]{1,0:T(8,128)}) %all-reduce.2.cloned.1.call-update) | async-done | bytes 393232 | tf_op jit(solution)/shard_map/psum | solution.py:46
  50.4 0.0 copy-done.2
  50.4 0.0 copy-done.4
  50.4 1.2 multiply_reduce_fusion.1
  51.6 11.7 %psum.22 = f32[96]{0:T(128)S(1)} all-reduce(f32[96]{0:T(128)S(1)} %multiply_reduce_fusion.1), channel_id=1, replica_groups=mesh['blocks'=2,'rows'=4,'cols'=4] {'rows'}, use_global_device_ids=true, to_apply=%region_2.3 | all-reduce | flops 96 | bytes 768 | tf_op jit(solution)/shard_map/psum | solution.py:48
  63.3 0.0 copy-start.3
  63.3 1.9 %fusion.31 = (bf16[96,1024]{1,0:T(8,128)(2,1)S(1)}, f32[96,1024]{1,0:T(8,128)}) fusion(f32[96]{0:T(128)S(1)} %add_sqrt_fusion.1, f32[96,1024]{1,0:T(8,128)} %all-reduce.2.cloned.1.call-done, f32[96,1024]{1,0:T(8,128)S(1)} %copy-done.2, f32[96]{0:T(128)S(1)} %copy-done.4), kind=kLoop, calls=%fused_computation.54 | loop fusion | flops 393216 | bytes 1377024 | tf_op jit(solution)/shard_map/convert_element_type | solution.py:51
  65.2 0.6 gather_fusion.1
  65.8 0.5 convolution_bitcast_fusion
  66.4 1.7 %fusion.4 = f32[96,8,256]{2,1,0:T(8,128)S(1)} fusion(f32[96,16,256]{2,0,1:T(8,128)S(1)} %convolution_bitcast_fusion, f32[16]{0:T(128)S(1)} %compare_convert_fusion, s32[16]{0:T(128)S(1)} %get-tuple-element.6), kind=kOutput, calls=%fused_computation.8 | convolution fusion | flops 37748992 | bytes 2359424 | tf_op jit(solution)/shard_map/ktj,ts->ksj/dot_general | solution.py:33
  68.1 1.0 all_gather_reshape.3
  69.1 0.0 all-gather.2.cloned.1.call-update
  69.1 0.0 copy-start.1
  69.1 60.8 %all-gather.2.cloned.1.call-done = f32[4,96,2048]{2,1,0:T(8,128)} async-done(((f32[1,96,2048]{2,1,0:T(8,128)}), f32[4,96,2048]{2,1,0:T(8,128)}) %all-gather.2.cloned.1.call-update) | async-done | bytes 3145744 | tf_op jit(solution)/shard_map/all_gather | solution.py:53
  129.9 3.1 %reduce_sum.28 = f32[96,2048]{1,0:T(8,128)} reduce(f32[4,96,2048]{2,1,0:T(8,128)} %all-gather.2.cloned.1.call-done, f32[]{:T(128)} %constant.32.clone.1), dimensions={0}, to_apply=%region_3.4 | reduce | flops 589824 | bytes 3932164 | tf_op jit(solution)/shard_map/reduce_sum | solution.py:53
  133.0 0.0 copy-done.1
  133.0 1.4 multiply_reduce_fusion
  134.4 6.4 %psum.23 = f32[96]{0:T(128)S(1)} all-reduce(f32[96]{0:T(128)S(1)} %multiply_reduce_fusion), channel_id=1, replica_groups=mesh['blocks'=2,'rows'=4,'cols'=4] {'cols'}, use_global_device_ids=true, to_apply=%region_5.6 | all-reduce | flops 96 | bytes 768 | tf_op jit(solution)/shard_map/psum | solution.py:55
  140.8 0.0 copy-done.3
  140.8 0.0 copy-start.5
  140.8 2.2 %broadcast_divide_fusion = f32[96,2048]{1,0:T(8,128)} fusion(f32[96]{0:T(128)S(1)} %add_sqrt_fusion, f32[96,2048]{1,0:T(8,128)} %reduce_sum.28, f32[96,2048]{1,0:T(8,128)S(1)} %copy-done.1, f32[96]{0:T(128)S(1)} %add_sqrt_fusion.1), kind=kLoop, calls=%fused_computation.20 | loop fusion | flops 589824 | bytes 2360064 | tf_op jit(solution)/shard_map/div | solution.py:57
  143.0 0.0 copy-done.5
  (6 shorter events, 0.1 us)
Async XLA Ops:
  7.2 4.2 %copy-start = (bf16[16,256,256]{2,1,0:T(8,128)(2,1)S(1)}, bf16[16,256,256]{2,1,0:T(8,128)(2,1)}, u32[]{:S(2)}) copy-start(bf16[16,256,256]{2,1,0:T(8,128)(2,1)} %param.6) | copy-start | bytes 6291460
  7.2 43.2 %all-reduce.2.cloned.1.call-start = ((), (), s32[]{:S(2)}) async-start(), calls=%async_computation | async-start | bytes 786432 | tf_op jit(solution)/shard_map/psum | solution.py:46
  12.1 38.3 %copy-start.2 = (f32[96,1024]{1,0:T(8,128)S(1)}, f32[96,1024]{1,0:T(8,128)}, u32[]{:S(2)}) copy-start(f32[96,1024]{1,0:T(8,128)} %param.9) | copy-start | bytes 1179652
  12.1 38.3 %copy-start.4 = (f32[96]{0:T(128)S(1)}, f32[96]{0:T(128)}, u32[]{:S(2)}) copy-start(f32[96]{0:T(128)} %param.11) | copy-start | bytes 1156
  14.7 115.2 %all-gather.2.cloned.1.call-start = ((), (), s32[]{:S(2)}) async-start(), calls=%async_computation.1 | async-start | bytes 3932160 | tf_op jit(solution)/shard_map/all_gather | solution.py:53
  63.3 77.5 %copy-start.3 = (f32[96]{0:T(128)}, f32[96]{0:T(128)S(1)}, u32[]{:S(2)}) copy-start(f32[96]{0:T(128)S(1)} %add_sqrt_fusion.1) | copy-start | bytes 1156
  69.1 63.9 %copy-start.1 = (f32[96,2048]{1,0:T(8,128)S(1)}, f32[96,2048]{1,0:T(8,128)}, u32[]{:S(2)}) copy-start(f32[96,2048]{1,0:T(8,128)} %param.10) | copy-start | bytes 2359300
  140.8 2.2 %copy-start.5 = (f32[96]{0:T(128)}, f32[96]{0:T(128)S(1)}, u32[]{:S(2)}) copy-start(f32[96]{0:T(128)S(1)} %add_sqrt_fusion) | copy-start | bytes 1156
Sparse Core Ops, SparseCore 0:
  14.8 35.5 all-reduce.1
  69.2 60.6 all-gather.1
